TPU v7x, 32 devices: a whole 2x2x4 slice. The times are simulated.
32 devices in a mesh: section: 2 (over core), shard: 4 (over y, x), replica: 4 (over z).
Axes of the slice: x: 2, y: 2, z: 4, core: 2. Of those that a mesh axis runs over, the one named last changes fastest.
Arguments:
- inputs: bfloat16 [8, 256, 960], P('replica', 'shard'), may hold values from -6 to 6
- cotangent: bfloat16 [8, 256, 960], P('replica', 'shard'), may hold values from -6 to 6
- segments: int32 [8, 256], P('replica'), may hold values from 0 to 3, never falling along the last dimension, each value on 1 to 128 neighbouring positions
- attn_q: bfloat16 [2, 960, 960], P('section', None, 'shard'), may hold values from -0.1875 to 0.1875
- attn_k: bfloat16 [2, 960, 320], P('section', None, 'shard'), may hold values from -0.1875 to 0.1875
- attn_v: bfloat16 [2, 960, 320], P('section', None, 'shard'), may hold values from -0.1875 to 0.1875
- attn_out: bfloat16 [2, 960, 960], P('section', None, 'shard'), may hold values from -0.75 to 0.75
- ffn_gate: bfloat16 [2, 960, 2560], P('section', None, 'shard'), may hold values from -0.1875 to 0.1875
- ffn_up: bfloat16 [2, 960, 2560], P('section', None, 'shard'), may hold values from -0.1875 to 0.1875
- ffn_down: bfloat16 [2, 2560, 960], P('section', 'shard'), may hold values from -0.125 to 0.125
- norm_gains: float32 [2, 2, 960], P('section'), may hold values from 0.1 to 1.9
Outputs:
- activations: bfloat16 [2, 8, 256, 960], P('section', 'replica', 'shard')
- input_grads: bfloat16 [2, 8, 256, 960], P('section', 'replica', 'shard')
- grad_q: float32 [2, 960, 960], P('section', 'replica', 'shard')
- grad_k: float32 [2, 960, 320], P('section', 'replica', 'shard')
- grad_v: float32 [2, 960, 320], P('section', 'replica', 'shard')
- grad_out: float32 [2, 960, 960], P('section', 'replica', 'shard')
- grad_gate: float32 [2, 960, 2560], P('section', 'replica', 'shard')
- grad_up: float32 [2, 960, 2560], P('section', 'replica', 'shard')
- grad_down: float32 [2, 2560, 960], P('section', 'shard', 'replica')
- grad_gains: float32 [2, 2, 960], P('section')
Inputs may be any that keep to these rules, and one draw needn't show every extreme that they name: `segments`: segment numbers never fall along a row, and every one of the 4 numbers occurs in every row.
All inputs are finite; a program needn't handle non-finite values.
Results may differ from a plain program's by a relative error of at most 0.024.
Values may be sent and summed in bfloat16 or wider, within the bound.
No kernel may reach another device: no remote copies, remote signals or barrier semaphores. Data moves between devices by JAX's collectives and lax.ppermute only.
A program may use at most 128 MiB of HBM per device.

v0:
```python
import jax
import jax.numpy as jnp
from jax import lax
from jax.sharding import PartitionSpec as P

HQ = 15
KV = 5
HD = 64


epsilon = 1e-05
rope_base = 10000.0
masked_score = -1e30


def from_behind(block, axis, distance):
    devices = range(lax.axis_size(axis))
    route = [(i - distance, i) for i in devices if i - distance in devices]
    return lax.ppermute(block, axis, route)


def matmul(left, right):
    return jnp.dot(left, right, preferred_element_type=jnp.float32)


def matmul_nt(left, right):
    return lax.dot_general(
        left, right, (((1,), (1,)), ((), ())), preferred_element_type=jnp.float32
    )


def matmul_tn(left, right):
    return lax.dot_general(
        left, right, (((0,), (0,)), ((), ())), preferred_element_type=jnp.float32
    )


def rope_tables(segments, head_dim):
    length = segments.shape[-1]
    position = jnp.arange(length, dtype=jnp.int32)
    before = jnp.concatenate([segments[:, :1] - 1, segments[:, :-1]], axis=1)
    starts = jnp.where(segments != before, position, 0)
    starts = lax.cummax(starts, axis=1)
    places = (position - starts).astype(jnp.float32)
    frequency = rope_base ** (jnp.arange(head_dim // 2, dtype=jnp.float32) * (-2.0 / head_dim))
    angles = places[..., None] * frequency
    return (jnp.cos(angles), jnp.sin(angles))


def rotate(values, cosine, sine_table):
    half_dim = values.shape[-1] // 2
    first_half = values[..., :half_dim]
    second_half = values[..., half_dim:]
    return jnp.concatenate(
        [
            first_half * cosine - second_half * sine_table,
            second_half * cosine + first_half * sine_table,
        ],
        axis=-1,
    )


def rotate_back(cotang, cosine, sine_table):
    half_dim = cotang.shape[-1] // 2
    first_half = cotang[..., :half_dim]
    second_half = cotang[..., half_dim:]
    return jnp.concatenate(
        [
            first_half * cosine + second_half * sine_table,
            second_half * cosine - first_half * sine_table,
        ],
        axis=-1,
    )


def score_block(queries, all_keys, allowed):
    scores = jnp.einsum(
        "qkrd,pkd->krqp", queries, all_keys, preferred_element_type=jnp.float32
    ) * queries.shape[-1] ** (-0.5)
    return jnp.where(allowed[None, None], scores, masked_score)


def attend_forward(queries, all_keys, all_values, allowed):
    scores = score_block(queries, all_keys, allowed)
    row_max = jnp.max(scores, axis=-1, keepdims=True)
    log_total = row_max + jnp.log(jnp.sum(jnp.exp(scores - row_max), axis=-1, keepdims=True))
    prob_rows = jnp.exp(scores - log_total).astype(jnp.bfloat16)
    attended = jnp.einsum(
        "krqp,pkd->qkrd", prob_rows, all_values, preferred_element_type=jnp.float32
    )
    return (log_total, attended.astype(jnp.bfloat16))


def attend_backward(queries, all_keys, all_values, allowed, log_total, attended, d_attended):
    scores = score_block(queries, all_keys, allowed)
    prob_full = jnp.exp(scores - log_total)
    prob_rows = prob_full.astype(jnp.bfloat16)
    d_probs = jnp.einsum(
        "qkrd,pkd->krqp", d_attended, all_values, preferred_element_type=jnp.float32
    )
    delta = jnp.einsum("qkrd,qkrd->krq", d_attended, attended, preferred_element_type=jnp.float32)
    d_scores = (prob_full * (d_probs - delta[..., None]) * queries.shape[-1] ** (-0.5)).astype(
        jnp.bfloat16
    )
    d_queries = jnp.einsum("krqp,pkd->qkrd", d_scores, all_keys, preferred_element_type=jnp.float32)
    key_part = jnp.einsum("krqp,qkrd->pkd", d_scores, queries, preferred_element_type=jnp.float32)
    value_part = jnp.einsum(
        "krqp,qkrd->pkd", prob_rows, d_attended, preferred_element_type=jnp.float32
    )
    return (d_queries, key_part, value_part)


def stack_ticks(pieces):
    return jax.tree.map(lambda *leaves: jnp.stack(leaves), *pieces)


def local(
    inputs,
    cotangent,
    segments,
    attn_q,
    attn_k,
    attn_v,
    attn_out,
    ffn_gate,
    ffn_up,
    ffn_down,
    norm_gains,
):
    section_at = lax.axis_index("section")
    block_at = lax.axis_index("shard")
    micro_count = inputs.shape[0]
    block_len = inputs.shape[1]
    model_width = inputs.shape[2]
    row_len = segments.shape[1]
    group_size = HQ // KV
    weight_q, weight_k, weight_v, weight_out = (
        lax.all_gather(attn_q[0], "shard", axis=1, tiled=True),
        lax.all_gather(attn_k[0], "shard", axis=1, tiled=True),
        lax.all_gather(attn_v[0], "shard", axis=1, tiled=True),
        lax.all_gather(attn_out[0], "shard", axis=1, tiled=True),
    )
    weight_gate = ffn_gate[0]
    weight_up = ffn_up[0]
    weight_down = ffn_down[0]
    gain_attn = norm_gains[0, 0]
    gain_ffn = norm_gains[0, 1]
    cos_rows, sin_rows = rope_tables(segments, HD)
    offset = block_at * block_len
    cos_own = lax.dynamic_slice_in_dim(cos_rows, offset, block_len, 1)
    sin_own = lax.dynamic_slice_in_dim(sin_rows, offset, block_len, 1)
    seg_own = lax.dynamic_slice_in_dim(segments, offset, block_len, 1)
    query_pos = offset + jnp.arange(block_len, dtype=jnp.int32)
    key_pos = jnp.arange(row_len, dtype=jnp.int32)
    allowed_all = (seg_own[:, :, None] == segments[:, None, :]) & (
        query_pos[:, None] >= key_pos[None, :]
    )[None]

    def micro_tables(micro_at):
        cosine = lax.dynamic_index_in_dim(cos_own, micro_at, 0, keepdims=False)[:, None, :]
        sine_table = lax.dynamic_index_in_dim(sin_own, micro_at, 0, keepdims=False)[:, None, :]
        allowed = lax.dynamic_index_in_dim(allowed_all, micro_at, 0, keepdims=False)
        return (cosine, sine_table, allowed)

    received = jnp.zeros((block_len, model_width), jnp.bfloat16)
    forward_saved = []
    forward_out = []
    for tick in range(micro_count + 1):
        own_input = inputs[min(tick, micro_count - 1)]
        layer_in = jnp.where(section_at == 0, own_input, received)
        micro_at = jnp.clip(tick - section_at, 0, micro_count - 1)
        forward_cosine, forward_sine_table, forward_allowed = micro_tables(micro_at)
        inputs_f = layer_in.astype(jnp.float32)
        inv_attn = lax.rsqrt(jnp.mean(inputs_f * inputs_f, axis=-1, keepdims=True) + epsilon)
        normed = (inputs_f * inv_attn * gain_attn).astype(jnp.bfloat16)
        queries = rotate(
            matmul(normed, weight_q).reshape(block_len, HQ, HD), forward_cosine, forward_sine_table
        ).astype(jnp.bfloat16)
        queries = queries.reshape(block_len, KV, group_size, HD)
        key_rows = rotate(
            matmul(normed, weight_k).reshape(block_len, KV, HD), forward_cosine, forward_sine_table
        ).astype(jnp.bfloat16)
        key_rows = key_rows.reshape(block_len, KV * HD)
        value_rows = matmul(normed, weight_v).astype(jnp.bfloat16)
        all_keys = lax.all_gather(key_rows, "shard", axis=0, tiled=True)
        all_values = lax.all_gather(value_rows, "shard", axis=0, tiled=True)
        all_keys = all_keys.reshape(row_len, KV, HD)
        all_values = all_values.reshape(row_len, KV, HD)
        log_total, attended = attend_forward(queries, all_keys, all_values, forward_allowed)
        attended_flat = attended.reshape(block_len, HQ * HD)
        middle = inputs_f + matmul(attended_flat, weight_out)
        inv_ffn = lax.rsqrt(jnp.mean(middle * middle, axis=-1, keepdims=True) + epsilon)
        normed_ffn = (middle * inv_ffn * gain_ffn).astype(jnp.bfloat16)
        rows_all = lax.all_gather(normed_ffn, "shard", axis=0, tiled=True)
        gate_pre = matmul(rows_all, weight_gate)
        up_pre = matmul(rows_all, weight_up)
        hidden = (jax.nn.silu(gate_pre) * up_pre).astype(jnp.bfloat16)
        ffn_sum = lax.psum_scatter(
            matmul(hidden, weight_down), "shard", scatter_dimension=0, tiled=True
        )
        layer_out = (middle + ffn_sum).astype(jnp.bfloat16)
        saved = (
            layer_in,
            inv_attn,
            normed,
            queries,
            all_keys,
            all_values,
            log_total,
            attended_flat,
            middle,
            inv_ffn,
            rows_all,
            gate_pre,
            up_pre,
            hidden,
        )
        layer_out, saved = (layer_out, saved)
        forward_out.append(layer_out)
        forward_saved.append(saved)
        if tick < micro_count:
            received = from_behind(layer_out, "section", 1)
    saved_stack = stack_ticks(forward_saved)
    received = jnp.zeros((block_len, model_width), jnp.bfloat16)
    backward_terms = []
    backward_out = []
    for tick in range(micro_count + 1):
        own_cot = cotangent[min(tick, micro_count - 1)]
        upstream = jnp.where(section_at == 1, own_cot, received)
        micro_at = jnp.clip(tick - 1 + section_at, 0, micro_count - 1)
        tick_saved = jax.tree.map(
            lambda stacked: lax.dynamic_index_in_dim(
                stacked, micro_at + section_at, 0, keepdims=False
            ),
            saved_stack,
        )
        (
            backward_layer_in,
            backward_inv_attn,
            backward_normed,
            backward_queries,
            backward_all_keys,
            backward_all_values,
            backward_log_total,
            backward_attended_flat,
            backward_middle,
            backward_inv_ffn,
            backward_rows_all,
            backward_gate_pre,
            backward_up_pre,
            backward_hidden,
        ) = tick_saved
        backward_cosine, backward_sine_table, backward_allowed = micro_tables(micro_at)
        grad_rows = lax.all_gather(upstream, "shard", axis=0, tiled=True)
        d_hidden = matmul_nt(grad_rows, weight_down)
        sigma = jax.nn.sigmoid(backward_gate_pre)
        d_gate = (
            d_hidden * backward_up_pre * sigma * (1.0 + backward_gate_pre * (1.0 - sigma))
        ).astype(jnp.bfloat16)
        d_up = (d_hidden * backward_gate_pre * sigma).astype(jnp.bfloat16)
        d_normed_ffn = lax.psum_scatter(
            matmul_nt(d_gate, weight_gate) + matmul_nt(d_up, weight_up),
            "shard",
            scatter_dimension=0,
            tiled=True,
        )
        scaled_ffn = d_normed_ffn * gain_ffn
        d_middle = (
            upstream.astype(jnp.float32)
            + backward_inv_ffn * scaled_ffn
            - backward_middle
            * (backward_inv_ffn * backward_inv_ffn * backward_inv_ffn)
            * jnp.mean(scaled_ffn * backward_middle, axis=-1, keepdims=True)
        )
        d_middle_b = d_middle.astype(jnp.bfloat16)
        d_attended = (
            matmul_nt(d_middle_b, weight_out)
            .astype(jnp.bfloat16)
            .reshape(block_len, KV, group_size, HD)
        )
        backward_attended = backward_attended_flat.reshape(block_len, KV, group_size, HD)
        d_queries, key_part, value_part = attend_backward(
            backward_queries,
            backward_all_keys,
            backward_all_values,
            backward_allowed,
            backward_log_total,
            backward_attended,
            d_attended,
        )
        d_keys = lax.psum_scatter(
            key_part.reshape(row_len, KV * HD), "shard", scatter_dimension=0, tiled=True
        )
        d_values = lax.psum_scatter(
            value_part.reshape(row_len, KV * HD), "shard", scatter_dimension=0, tiled=True
        )
        d_q_rot = (
            rotate_back(d_queries.reshape(block_len, HQ, HD), backward_cosine, backward_sine_table)
            .reshape(block_len, HQ * HD)
            .astype(jnp.bfloat16)
        )
        d_k_rot = (
            rotate_back(d_keys.reshape(block_len, KV, HD), backward_cosine, backward_sine_table)
            .reshape(block_len, KV * HD)
            .astype(jnp.bfloat16)
        )
        d_v_rows = d_values.astype(jnp.bfloat16)
        d_normed = (
            matmul_nt(d_q_rot, weight_q)
            + matmul_nt(d_k_rot, weight_k)
            + matmul_nt(d_v_rows, weight_v)
        )
        backward_inputs_f = backward_layer_in.astype(jnp.float32)
        scaled_attn = d_normed * gain_attn
        d_inputs = (
            d_middle
            + backward_inv_attn * scaled_attn
            - backward_inputs_f
            * (backward_inv_attn * backward_inv_attn * backward_inv_attn)
            * jnp.mean(scaled_attn * backward_inputs_f, axis=-1, keepdims=True)
        )
        gain_terms = jnp.stack(
            [
                jnp.sum(d_normed * backward_inputs_f * backward_inv_attn, axis=0),
                jnp.sum(d_normed_ffn * backward_middle * backward_inv_ffn, axis=0),
            ]
        )
        d_inputs, terms = (
            d_inputs.astype(jnp.bfloat16),
            (grad_rows, d_gate, d_up, d_middle_b, d_q_rot, d_k_rot, d_v_rows, gain_terms),
        )
        backward_out.append(d_inputs)
        backward_terms.append(terms)
        if tick < micro_count:
            received = from_behind(d_inputs, "section", -1)
    terms_stack = stack_ticks(backward_terms)

    def forward_rows(stacked):
        return lax.dynamic_slice_in_dim(stacked, section_at, micro_count, 0)

    def backward_rows(stacked):
        return lax.dynamic_slice_in_dim(stacked, 1 - section_at, micro_count, 0)

    layer_acts = forward_rows(jnp.stack(forward_out))
    layer_grads = backward_rows(jnp.stack(backward_out))
    own_tokens = micro_count * block_len
    row_tokens = micro_count * row_len
    ffn_rows_all = forward_rows(saved_stack[10]).reshape(row_tokens, model_width)
    hidden_all = forward_rows(saved_stack[13])
    hidden_all = hidden_all.reshape(row_tokens, hidden_all.shape[-1])
    grad_rows_all = backward_rows(terms_stack[0]).reshape(row_tokens, model_width)
    d_gate_all = backward_rows(terms_stack[1])
    d_gate_all = d_gate_all.reshape(row_tokens, d_gate_all.shape[-1])
    d_up_all = backward_rows(terms_stack[2])
    d_up_all = d_up_all.reshape(row_tokens, d_up_all.shape[-1])
    gains_local = jnp.sum(backward_rows(terms_stack[7]), axis=0)
    grad_gate_local = matmul_tn(ffn_rows_all, d_gate_all)
    grad_up_local = matmul_tn(ffn_rows_all, d_up_all)
    grad_down_local = matmul_tn(hidden_all, grad_rows_all)
    normed_all = forward_rows(saved_stack[2]).reshape(own_tokens, model_width)
    attended_all = forward_rows(saved_stack[7]).reshape(own_tokens, HQ * HD)
    d_middle_all = backward_rows(terms_stack[3]).reshape(own_tokens, model_width)
    d_q_all = backward_rows(terms_stack[4]).reshape(own_tokens, HQ * HD)
    d_k_all = backward_rows(terms_stack[5]).reshape(own_tokens, KV * HD)
    d_v_all = backward_rows(terms_stack[6]).reshape(own_tokens, KV * HD)
    grad_q_local = matmul_tn(normed_all, d_q_all)
    grad_k_local = matmul_tn(normed_all, d_k_all)
    grad_v_local = matmul_tn(normed_all, d_v_all)
    grad_out_local = matmul_tn(attended_all, d_middle_all)
    owned_q, owned_k, owned_v, owned_out = (
        lax.psum_scatter(grad_q_local, "shard", scatter_dimension=1, tiled=True),
        lax.psum_scatter(grad_k_local, "shard", scatter_dimension=1, tiled=True),
        lax.psum_scatter(grad_v_local, "shard", scatter_dimension=1, tiled=True),
        lax.psum_scatter(grad_out_local, "shard", scatter_dimension=1, tiled=True),
    )
    summed = (
        lax.psum_scatter(owned_q, "replica", scatter_dimension=0, tiled=True),
        lax.psum_scatter(owned_k, "replica", scatter_dimension=0, tiled=True),
        lax.psum_scatter(owned_v, "replica", scatter_dimension=0, tiled=True),
        lax.psum_scatter(owned_out, "replica", scatter_dimension=0, tiled=True),
        lax.psum_scatter(grad_gate_local, "replica", scatter_dimension=0, tiled=True),
        lax.psum_scatter(grad_up_local, "replica", scatter_dimension=0, tiled=True),
        lax.psum_scatter(grad_down_local, "replica", scatter_dimension=1, tiled=True),
    )
    final_q, final_k, final_v, final_out, final_gate, final_up, final_down = summed
    gains_total = lax.psum(gains_local, ("shard", "replica"))
    return (
        layer_acts[None],
        layer_grads[None],
        final_q[None],
        final_k[None],
        final_v[None],
        final_out[None],
        final_gate[None],
        final_up[None],
        final_down[None],
        gains_total[None],
    )


def solution(mesh):
    placed = (
        P("replica", "shard", None),
        P("replica", "shard", None),
        P("replica", None),
        P("section", None, "shard"),
        P("section", None, "shard"),
        P("section", None, "shard"),
        P("section", None, "shard"),
        P("section", None, "shard"),
        P("section", None, "shard"),
        P("section", "shard", None),
        P("section", None, None),
    )
    return jax.shard_map(
        local,
        mesh=mesh,
        in_specs=placed,
        out_specs=(
            P("section", "replica", "shard", None),
            P("section", "replica", "shard", None),
            P("section", "replica", "shard"),
            P("section", "replica", "shard"),
            P("section", "replica", "shard"),
            P("section", "replica", "shard"),
            P("section", "replica", "shard"),
            P("section", "replica", "shard"),
            P("section", "shard", "replica"),
            P("section", None, None),
        ),
        check_vma=False,
    )
```

profile of v0, /device:TPU:0, one launch (start us, length us, event | category | flops | bytes accessed | tf_op | source)
XLA Modules:
  0.0 1143.9 jit_solution(6483214833668729290)
XLA Ops:
  14.8 15.6 %all-gather.1 = bf16[1,960,320]{1,2,0:T(8,128)(2,1)S(1)} all-gather(bf16[1,960,80]{1,2,0:T(8,128)(2,1)S(1)} %copy-done.139), channel_id=3, replica_groups=mesh['section'=2,'shard'=4,'replica'=4] {'shard'}, dimensions={2}, use_global_device_ids=true | all-gather | bytes 768000 | tf_op jit(solution)/shard_map/all_gather | solution.py:139
  32.0 9.7 all_gather.51
  41.9 15.5 %all-gather = bf16[1,960,320]{1,2,0:T(8,128)(2,1)S(1)} all-gather(bf16[1,960,80]{1,2,0:T(8,128)(2,1)S(1)} %copy-done.140), channel_id=2, replica_groups=mesh['section'=2,'shard'=4,'replica'=4] {'shard'}, dimensions={2}, use_global_device_ids=true | all-gather | bytes 768000 | tf_op jit(solution)/shard_map/all_gather | solution.py:140
  57.8 11.1 all_gather.49
  78.5 46.4 %all-gather.10.cloned.1.call-done = bf16[1,960,960]{1,0,2:T(2,128)(2,1)} async-done(((bf16[1,960,240]{1,0,2:T(2,128)(2,1)}), bf16[1,960,960]{1,0,2:T(2,128)(2,1)}) %all-gather.10.cloned.1.call-update) | async-done | bytes 1843216 | tf_op jit(solution)/shard_map/all_gather | solution.py:141
  135.8 10.1 all_gather.54
  150.4 28.0 %reduce-scatter.38.cloned.1.call-done = f32[64,960]{1,0:T(8,128)} async-done(((f32[256,960]{1,0:T(8,128)}), f32[64,960]{1,0:T(8,128)}) %reduce-scatter.38.cloned.1.call-update) | async-done | bytes 245776 | tf_op jit(solution)/shard_map/reduce_scatter | solution.py:198
  183.0 10.5 copy.351
  232.1 10.4 all_gather.57
  247.0 28.0 %reduce-scatter.40.cloned.1.call-done = f32[64,960]{1,0:T(8,128)} async-done(((f32[256,960]{1,0:T(8,128)}), f32[64,960]{1,0:T(8,128)}) %reduce-scatter.40.cloned.1.call-update) | async-done | bytes 245776 | tf_op jit(solution)/shard_map/reduce_scatter | solution.py:198
  281.3 11.1 all-gather.4
  333.3 9.9 all_gather.60
  426.6 22.1 %reduce-scatter.46.cloned.1.call-done = f32[64,320]{1,0:T(8,128)} async-done(((f32[256,320]{1,0:T(8,128)}), f32[64,320]{1,0:T(8,128)}) %reduce-scatter.46.cloned.1.call-update) | async-done | bytes 81936 | tf_op jit(solution)/shard_map/reduce_scatter | solution.py:294
  455.5 10.0 all_gather.62
  476.3 22.0 %reduce-scatter.48.cloned.1.call-done = f32[64,960]{1,0:T(8,128)} async-done(((f32[256,960]{1,0:T(8,128)}), f32[64,960]{1,0:T(8,128)}) %reduce-scatter.48.cloned.1.call-update) | async-done | bytes 245776 | tf_op jit(solution)/shard_map/reduce_scatter | solution.py:261
  527.3 11.1 reduce-scatter.72.cloned.1.call-done
  543.8 21.9 %reduce-scatter.50.cloned.1.call-done = f32[64,320]{1,0:T(8,128)} async-done(((f32[256,320]{1,0:T(8,128)}), f32[64,320]{1,0:T(8,128)}) %reduce-scatter.50.cloned.1.call-update) | async-done | bytes 81936 | tf_op jit(solution)/shard_map/reduce_scatter | solution.py:294
  572.9 10.0 all_gather.63
  590.9 24.8 %reduce-scatter.52.cloned.1.call-done = f32[64,960]{1,0:T(8,128)} async-done(((f32[256,960]{1,0:T(8,128)}), f32[64,960]{1,0:T(8,128)}) %reduce-scatter.52.cloned.1.call-update) | async-done | bytes 245776 | tf_op jit(solution)/shard_map/reduce_scatter | solution.py:261
  628.5 20.6 %reduce-scatter.54.cloned.1.call-done = f32[64,320]{1,0:T(8,128)} async-done(((f32[256,320]{1,0:T(8,128)}), f32[64,320]{1,0:T(8,128)}) %reduce-scatter.54.cloned.1.call-update) | async-done | bytes 81936 | tf_op jit(solution)/shard_map/reduce_scatter | solution.py:294
  651.9 24.9 %reduce-scatter.74.cloned.1.call-done = f32[64,320]{1,0:T(8,128)} async-done(((f32[256,320]{1,0:T(8,128)}), f32[64,320]{1,0:T(8,128)}) %reduce-scatter.74.cloned.1.call-update) | async-done | bytes 81936
  693.8 15.2 %reduce-scatter.60.cloned.1.call-done = f32[960,80]{0,1:T(8,128)} async-done(((f32[960,320]{0,1:T(8,128)}), f32[960,80]{0,1:T(8,128)}) %reduce-scatter.60.cloned.1.call-update) | async-done | bytes 307216 | tf_op jit(solution)/shard_map/reduce_scatter | solution.py:373
  711.1 30.3 %reduce-scatter.58.cloned.1.call-done = f32[960,80]{0,1:T(8,128)} async-done(((f32[960,320]{0,1:T(8,128)}), f32[960,80]{0,1:T(8,128)}) %reduce-scatter.58.cloned.1.call-update) | async-done | bytes 307216 | tf_op jit(solution)/shard_map/reduce_scatter | solution.py:372
  758.0 36.7 %reduce-scatter.82.cloned.1.call-done = f32[240,960]{1,0:T(8,128)} async-done(((f32[960,960]{1,0:T(8,128)}), f32[240,960]{1,0:T(8,128)}) %reduce-scatter.82.cloned.1.call-update) | async-done | bytes 921616
  797.3 28.2 %reduce-scatter.42.cloned.1.call-done = f32[64,960]{1,0:T(8,128)} async-done(((f32[256,960]{1,0:T(8,128)}), f32[64,960]{1,0:T(8,128)}) %reduce-scatter.42.cloned.1.call-update) | async-done | bytes 245776 | tf_op jit(solution)/shard_map/reduce_scatter | solution.py:198
  827.1 51.7 %reduce-scatter.76.cloned.1.call-done = f32[240,960]{1,0:T(8,128)} async-done(((f32[960,960]{1,0:T(8,128)}), f32[240,960]{1,0:T(8,128)}) %reduce-scatter.76.cloned.1.call-update) | async-done | bytes 921616
  889.7 42.6 %psum.7 = f32[1,2,960]{2,1,0:T(2,128)} all-reduce(f32[1,2,960]{2,1,0:T(2,128)S(1)} %bitcast.958), channel_id=1, replica_groups=mesh['section'=2,'shard'=4,'replica'=4] {'shard','replica'}, use_global_device_ids=true, to_apply=%region_50.51 | all-reduce | flops 1920 | bytes 15360 | tf_op jit(solution)/shard_map/psum | solution.py:386
  937.4 39.0 %reduce-scatter.68.cloned.1.call-done = f32[640,240]{0,1:T(8,128)} async-done(((f32[640,960]{0,1:T(8,128)}), f32[640,240]{0,1:T(8,128)}) %reduce-scatter.68.cloned.1.call-update) | async-done | bytes 614416 | tf_op jit(solution)/shard_map/reduce_scatter | solution.py:383
  976.5 52.1 %reduce-scatter.66.cloned.1.call-done = f32[240,640]{1,0:T(8,128)} async-done(((f32[960,640]{1,0:T(8,128)}), f32[240,640]{1,0:T(8,128)}) %reduce-scatter.66.cloned.1.call-update) | async-done | bytes 614416 | tf_op jit(solution)/shard_map/reduce_scatter | solution.py:382
  1028.6 52.1 %reduce-scatter.64.cloned.1.call-done = f32[240,640]{1,0:T(8,128)} async-done(((f32[960,640]{1,0:T(8,128)}), f32[240,640]{1,0:T(8,128)}) %reduce-scatter.64.cloned.1.call-update) | async-done | bytes 614416 | tf_op jit(solution)/shard_map/reduce_scatter | solution.py:381
  1080.7 28.5 %reduce-scatter.62.cloned.1.call-done = f32[240,240]{1,0:T(8,128)} async-done(((f32[960,240]{1,0:T(8,128)}), f32[240,240]{1,0:T(8,128)}) %reduce-scatter.62.cloned.1.call-update) | async-done | bytes 230416 | tf_op jit(solution)/shard_map/reduce_scatter | solution.py:380
  1109.2 27.7 %reduce-scatter.56.cloned.1.call-done = f32[240,240]{1,0:T(8,128)} async-done(((f32[960,240]{1,0:T(8,128)}), f32[240,240]{1,0:T(8,128)}) %reduce-scatter.56.cloned.1.call-update) | async-done | bytes 230416 | tf_op jit(solution)/shard_map/reduce_scatter | solution.py:377
  (677 shorter events, 349.5 us)
Async XLA Ops:
  7.2 65.0 %all-gather.8.cloned.1.call-start = ((), (), s32[]{:S(2)}) async-start(), calls=%async_computation.39 | async-start | bytes 4915200 | tf_op jit(solution)/shard_map/all_gather | solution.py:138
  11.0 113.8 %all-gather.10.cloned.1.call-start = ((), (), s32[]{:S(2)}) async-start(), calls=%async_computation.40 | async-start | bytes 4915200 | tf_op jit(solution)/shard_map/all_gather | solution.py:141
  13.2 165.2 %reduce-scatter.38.cloned.1.call-start = ((), (), s32[]{:S(2)}) async-start(), calls=%async_computation.23 | async-start | bytes 1310720 | tf_op jit(solution)/shard_map/reduce_scatter | solution.py:198
  31.9 149.8 %copy-start.147 = (f32[64,32]{0,1:T(8,128)}, f32[64,32]{0,1:T(8,128)S(1)}, u32[]{:S(2)}) copy-start(f32[64,32]{0,1:T(8,128)S(1)} %get-tuple-element.89) | copy-start | bytes 24580
  31.9 150.5 %copy-start.149 = (f32[64,32]{0,1:T(8,128)}, f32[64,32]{0,1:T(8,128)S(1)}, u32[]{:S(2)}) copy-start(f32[64,32]{0,1:T(8,128)S(1)} %get-tuple-element.155) | copy-start | bytes 24580
  31.9 248.1 %copy-start.143 = (f32[64,32]{0,1:T(8,128)}, f32[64,32]{0,1:T(8,128)S(1)}, u32[]{:S(2)}) copy-start(f32[64,32]{0,1:T(8,128)S(1)} %get-tuple-element.88) | copy-start | bytes 24580
  150.3 124.7 %reduce-scatter.40.cloned.1.call-start = ((), (), s32[]{:S(2)}) async-start(), calls=%async_computation.24 | async-start | bytes 1310720 | tf_op jit(solution)/shard_map/reduce_scatter | solution.py:198
  180.1 13.5 %collective-permute-start = (bf16[64,960]{1,0:T(8,128)(2,1)}, bf16[64,960]{1,0:T(8,128)(2,1)S(1)}, u32[]{:S(2)}, u32[]{:S(2)}) collective-permute-start(bf16[64,960]{1,0:T(8,128)(2,1)} %add_convert_fusion.4), channel_id=1, source_target_pairs={{0,16},{1,17},{2,18},{3,19},{4,20},{5,21},{6,22},{7,23},{8,24},{9,... | collective-permute-start | bytes 368648 | tf_op jit(solution)/shard_map/ppermute | solution.py:19
  247.0 133.9 %reduce-scatter.44.cloned.1.call-start = ((), (), s32[]{:S(2)}) async-start(), calls=%async_computation.26 | async-start | bytes 1310720 | tf_op jit(solution)/shard_map/reduce_scatter | solution.py:261
  276.7 15.6 %collective-permute-start.1 = (bf16[64,960]{1,0:T(8,128)(2,1)}, bf16[64,960]{1,0:T(8,128)(2,1)}, u32[]{:S(2)}, u32[]{:S(2)}) collective-permute-start(bf16[64,960]{1,0:T(8,128)(2,1)} %add_convert_fusion.3), channel_id=1, source_target_pairs={{0,16},{1,17},{2,18},{3,19},{4,20},{5,21},{6,22},{7,23},{8,24},{9,... | collective-permute-start | bytes 368648 | tf_op jit(solution)/shard_map/ppermute | solution.py:19
  352.2 68.9 %reduce-scatter.70.cloned.1.call-start = ((), (), s32[]{:S(2)}) async-start(), calls=%async_computation.41 | async-start | bytes 491520
  396.3 52.4 %reduce-scatter.46.cloned.1.call-start = ((), (), s32[]{:S(2)}) async-start(), calls=%async_computation.27 | async-start | bytes 491520 | tf_op jit(solution)/shard_map/reduce_scatter | solution.py:294
  410.4 88.0 %reduce-scatter.48.cloned.1.call-start = ((), (), s32[]{:S(2)}) async-start(), calls=%async_computation.28 | async-start | bytes 1310720 | tf_op jit(solution)/shard_map/reduce_scatter | solution.py:261
  452.3 3.2 collective-permute-start.2
  470.2 68.1 %reduce-scatter.72.cloned.1.call-start = ((), (), s32[]{:S(2)}) async-start(), calls=%async_computation.42 | async-start | bytes 491520
  513.5 52.3 %reduce-scatter.50.cloned.1.call-start = ((), (), s32[]{:S(2)}) async-start(), calls=%async_computation.29 | async-start | bytes 491520 | tf_op jit(solution)/shard_map/reduce_scatter | solution.py:294
  524.1 91.6 %reduce-scatter.52.cloned.1.call-start = ((), (), s32[]{:S(2)}) async-start(), calls=%async_computation.30 | async-start | bytes 1310720 | tf_op jit(solution)/shard_map/reduce_scatter | solution.py:261
  569.0 3.2 collective-permute-start.3
  587.6 61.6 %reduce-scatter.54.cloned.1.call-start = ((), (), s32[]{:S(2)}) async-start(), calls=%async_computation.31 | async-start | bytes 491520 | tf_op jit(solution)/shard_map/reduce_scatter | solution.py:294
  624.3 52.4 %reduce-scatter.74.cloned.1.call-start = ((), (), s32[]{:S(2)}) async-start(), calls=%async_computation.43 | async-start | bytes 491520
  628.3 80.8 %reduce-scatter.60.cloned.1.call-start = ((), (), s32[]{:S(2)}) async-start(), calls=%async_computation.34 | async-start | bytes 1638400 | tf_op jit(solution)/shard_map/reduce_scatter | solution.py:373
  651.6 89.8 %reduce-scatter.58.cloned.1.call-start = ((), (), s32[]{:S(2)}) async-start(), calls=%async_computation.33 | async-start | bytes 1638400 | tf_op jit(solution)/shard_map/reduce_scatter | solution.py:372
  679.5 115.2 %reduce-scatter.82.cloned.1.call-start = ((), (), s32[]{:S(2)}) async-start(), calls=%async_computation.47 | async-start | bytes 4915200
  682.3 143.1 %reduce-scatter.42.cloned.1.call-start = ((), (), s32[]{:S(2)}) async-start(), calls=%async_computation.25 | async-start | bytes 1310720 | tf_op jit(solution)/shard_map/reduce_scatter | solution.py:198
  686.2 192.6 %reduce-scatter.76.cloned.1.call-start = ((), (), s32[]{:S(2)}) async-start(), calls=%async_computation.44 | async-start | bytes 4915200
  693.5 240.7 %reduce-scatter.80.cloned.1.call-start = ((), (), s32[]{:S(2)}) async-start(), calls=%async_computation.46 | async-start | bytes 614400
  711.0 224.8 %reduce-scatter.78.cloned.1.call-start = ((), (), s32[]{:S(2)}) async-start(), calls=%async_computation.45 | async-start | bytes 614400
  743.3 233.2 %reduce-scatter.68.cloned.1.call-start = ((), (), s32[]{:S(2)}) async-start(), calls=%async_computation.38 | async-start | bytes 3072000 | tf_op jit(solution)/shard_map/reduce_scatter | solution.py:383
  747.6 281.0 %reduce-scatter.66.cloned.1.call-start = ((), (), s32[]{:S(2)}) async-start(), calls=%async_computation.37 | async-start | bytes 3072000 | tf_op jit(solution)/shard_map/reduce_scatter | solution.py:382
  753.1 327.6 %reduce-scatter.64.cloned.1.call-start = ((), (), s32[]{:S(2)}) async-start(), calls=%async_computation.36 | async-start | bytes 3072000 | tf_op jit(solution)/shard_map/reduce_scatter | solution.py:381
  758.0 351.2 %reduce-scatter.62.cloned.1.call-start = ((), (), s32[]{:S(2)}) async-start(), calls=%async_computation.35 | async-start | bytes 1228800 | tf_op jit(solution)/shard_map/reduce_scatter | solution.py:380
  797.2 339.7 %reduce-scatter.56.cloned.1.call-start = ((), (), s32[]{:S(2)}) async-start(), calls=%async_computation.32 | async-start | bytes 1228800 | tf_op jit(solution)/shard_map/reduce_scatter | solution.py:377
  (175 other events, 1647.3 us)
Sparse Core Ops, SparseCore 0:
  11.1 61.0 all-gather.7
  74.0 50.7 all-gather.9
  150.5 27.9 reduce-scatter.37
  247.1 27.8 reduce-scatter.39
  352.3 27.9 reduce-scatter.43
  396.4 24.7 reduce-scatter.69
  423.9 24.7 reduce-scatter.45
  470.4 27.9 reduce-scatter.47
  513.6 24.7 reduce-scatter.71
  541.0 24.6 reduce-scatter.49
  587.7 27.9 reduce-scatter.51
  624.4 24.7 reduce-scatter.53
  652.0 24.6 reduce-scatter.73
  679.5 29.4 reduce-scatter.59
  711.8 29.4 reduce-scatter.57
  744.2 50.4 reduce-scatter.81
  797.5 27.9 reduce-scatter.41
  828.4 50.4 reduce-scatter.75
  881.1 21.7 reduce-scatter.79
  905.0 20.3 reduce-scatter.77
  928.4 48.0 reduce-scatter.67
  979.4 49.1 reduce-scatter.65
  1031.5 49.1 reduce-scatter.63
  1083.4 25.7 reduce-scatter.61
  1112.1 24.7 reduce-scatter.55
where the time goes:
time: 1160 us; the launch traced here: 1140 us
  waiting for transfers between devices  626 us (54%)
  blocking collectives  191 us (16%)
  local copies, waits for them, and re-layouts  136 us (12%)
  matrix products  113 us (10%)
  other arithmetic  53.3 us (5%)
  between operations  16.7 us (1%)
    unnamed x32, waiting for transfers between devices  132 us
    reduce_scatter x3, waiting for transfers between devices, local(): lax.psum_scatter(matmul(hidden, weight_down), 'shard', scatter_dimension=...  84.2 us
    reduce_scatter x3, waiting for transfers between devices, local(): lax.psum_scatter(value_part.reshape(row_len, KV * HD), 'shard', scatter_d...  64.6 us
    unnamed x379, local copies, waits for them, and re-layouts  58.2 us
    reduce_scatter x1, waiting for transfers between devices, local(): lax.psum_scatter(grad_gate_local, 'replica', scatter_dimension=0, tiled=T...  52.1 us
    reduce_scatter x1, waiting for transfers between devices, local(): lax.psum_scatter(grad_up_local, 'replica', scatter_dimension=0, tiled=True)  52.1 us
    reduce_scatter x3, waiting for transfers between devices, local(): lax.psum_scatter(matmul_nt(d_gate, weight_gate) + matmul_nt(d_up, weight_...  46.8 us
    all_gather x1, waiting for transfers between devices, local(): lax.all_gather(attn_out[0], 'shard', axis=1, tiled=True)  46.4 us
  transfers between devices with their start and end apart: 29, of which 24 were waited for; matrix products, arithmetic and copies ran while one was open for 14% of the time, Pallas kernels for 0%

commit v1 on v0

v1 whole, which is shorter than its diff:
```python
import functools

import jax
import jax.numpy as jnp
from jax import lax
from jax.experimental import pallas as pl
from jax.experimental.pallas import tpu as pltpu
from jax.sharding import PartitionSpec as P

HQ = 15
KV = 5
HD = 64
GROUP = HQ // KV
epsilon = 1e-05
rope_base = 10000.0
masked_score = -1e30
F32 = jnp.float32
BF16 = jnp.bfloat16


def dot(left, right):
    return lax.dot_general(left, right, (((1,), (0,)), ((), ())), preferred_element_type=F32)


def dot_nt(left, right):
    return lax.dot_general(left, right, (((1,), (1,)), ((), ())), preferred_element_type=F32)


def dot_tn(left, right):
    return lax.dot_general(left, right, (((0,), (0,)), ((), ())), preferred_element_type=F32)


def wide(table, width):
    copies = -(-width // table.shape[1])
    return jnp.concatenate([table] * copies, axis=1)[:, :width]


def swap_halves(values):
    half = HD // 2
    up = jnp.concatenate([values[:, half:], values[:, :half]], axis=1)
    down = jnp.concatenate([values[:, -half:], values[:, :-half]], axis=1)
    lane = lax.broadcasted_iota(jnp.int32, values.shape, 1)
    return jnp.where(lane % HD < half, up, down)


def rope(values, cosine, sine, sign):
    width = values.shape[1]
    turned = swap_halves(values) * wide(sine, width)
    straight = values * wide(cosine, width)
    return straight + turned if sign > 0 else straight - turned


def forward_kernel(at_ref, u_ref, w_ref, gate_ref, up_ref, down_ref, gain_ref, cos_ref, sin_ref,
                   seg_c_ref, pos_c_ref, seg_r_ref, pos_r_ref,
                   part_ref, normed_ref, q_ref, k_ref, v_ref, prob_ref, att_ref, mid_ref, nffn_ref,
                   gpre_ref, upre_ref, hid_ref, qf_ref, kf_ref):
    at = at_ref[0]
    count = w_ref.shape[0]
    width = u_ref.shape[1]
    qw = HQ * HD // count
    kw = KV * HD // count
    u = u_ref[...].astype(F32)
    inv_a = lax.rsqrt(jnp.mean(u * u, axis=-1, keepdims=True) + epsilon)
    normed = (u * inv_a * gain_ref[0:1, :]).astype(BF16)
    normed_ref[...] = normed
    for c in range(count):
        rc = lax.rem(at - c + count, count)
        qkv = dot(normed, w_ref[rc, :, : qw + 2 * kw])
        qf_ref[:, c * qw : (c + 1) * qw] = qkv[:, :qw]
        kf_ref[:, c * kw : (c + 1) * kw] = qkv[:, qw : qw + kw]
        v_ref[:, c * kw : (c + 1) * kw] = qkv[:, qw + kw :].astype(BF16)
    cosine = cos_ref[...]
    sine = sin_ref[...]
    q_ref[...] = rope(qf_ref[...], cosine, sine, 1).astype(BF16)
    k_ref[...] = rope(kf_ref[...], cosine, sine, 1).astype(BF16)
    allowed = (seg_c_ref[...] == seg_r_ref[...]) & (pos_c_ref[...] >= pos_r_ref[...])
    for h in range(KV):
        keys = k_ref[:, h * HD : (h + 1) * HD]
        vals = v_ref[:, h * HD : (h + 1) * HD]
        for g in range(GROUP):
            hd = h * GROUP + g
            scores = dot_nt(q_ref[:, hd * HD : (hd + 1) * HD], keys) * HD ** (-0.5)
            scores = jnp.where(allowed, scores, masked_score)
            e = jnp.exp(scores - jnp.max(scores, axis=-1, keepdims=True))
            prob = (e / jnp.sum(e, axis=-1, keepdims=True)).astype(BF16)
            prob_ref[hd] = prob
            att_ref[:, hd * HD : (hd + 1) * HD] = dot(prob, vals).astype(BF16)
    attended = att_ref[...]
    cw = width // count
    for c in range(count):
        rc = lax.rem(at - c + count, count)
        mid_ref[:, c * cw : (c + 1) * cw] = dot(attended, w_ref[rc, :, qw + 2 * kw :])
    middle = u + mid_ref[...]
    mid_ref[...] = middle
    inv_f = lax.rsqrt(jnp.mean(middle * middle, axis=-1, keepdims=True) + epsilon)
    nffn = (middle * inv_f * gain_ref[1:2, :]).astype(BF16)
    nffn_ref[...] = nffn
    gpre = dot(nffn, gate_ref[...])
    upre = dot(nffn, up_ref[...])
    gpre_ref[...] = gpre
    upre_ref[...] = upre
    hidden = (gpre * jax.nn.sigmoid(gpre) * upre).astype(BF16)
    hid_ref[...] = hidden
    part_ref[...] = dot(hidden, down_ref[...]).astype(BF16)


def ffn_back_kernel(g_ref, gpre_ref, upre_ref, gate_ref, up_ref, down_ref, dgu_ref, part_ref):
    d_hidden = dot_nt(g_ref[...], down_ref[...])
    gpre = gpre_ref[...]
    sigma = jax.nn.sigmoid(gpre)
    d_gate = (d_hidden * upre_ref[...] * sigma * (1.0 + gpre * (1.0 - sigma))).astype(BF16)
    d_up = (d_hidden * gpre * sigma).astype(BF16)
    hidden = d_gate.shape[1]
    dgu_ref[:, :hidden] = d_gate
    dgu_ref[:, hidden:] = d_up
    part_ref[...] = (dot_nt(d_gate, gate_ref[...]) + dot_nt(d_up, up_ref[...])).astype(BF16)


def attn_back_kernel(at_ref, dmid_ref, u_ref, w_ref, gain_ref, cos_ref, sin_ref, q_ref, k_ref, v_ref,
                     prob_ref, att_ref,
                     din_ref, dqkv_ref, dmo_ref, gsum_ref, datt_ref, dq_ref, dk_ref, dv_ref, piece_ref, *, own):
    at = at_ref[0]
    count = w_ref.shape[0]
    width = u_ref.shape[1]
    qw = HQ * HD // count
    kw = KV * HD // count
    cw = width // count
    dmid = dmid_ref[...]
    d_att = jnp.zeros((dmid.shape[0], HQ * HD), F32)
    for c in range(count):
        rc = lax.rem(at - c + count, count)
        d_att = d_att + dot_nt(dmid[:, c * cw : (c + 1) * cw], w_ref[rc, :, qw + 2 * kw :])

        @pl.when(at == c)
        def _():
            dmo_ref[...] = dmid[:, c * cw : (c + 1) * cw]

    datt_ref[...] = d_att.astype(BF16)
    for h in range(KV):
        keys = k_ref[:, h * HD : (h + 1) * HD]
        vals = v_ref[:, h * HD : (h + 1) * HD]
        d_k = jnp.zeros((dmid.shape[0], HD), F32)
        d_v = jnp.zeros((dmid.shape[0], HD), F32)
        for g in range(GROUP):
            hd = h * GROUP + g
            span = slice(hd * HD, (hd + 1) * HD)
            da = datt_ref[:, span]
            prob = prob_ref[hd]
            d_prob = dot_nt(da, vals)
            delta = jnp.sum(da.astype(F32) * att_ref[:, span].astype(F32), axis=-1, keepdims=True)
            d_s = (prob.astype(F32) * (d_prob - delta) * HD ** (-0.5)).astype(BF16)
            dq_ref[:, span] = dot(d_s, keys)
            d_k = d_k + dot_tn(d_s, q_ref[:, span])
            d_v = d_v + dot_tn(prob, da)
        dk_ref[:, h * HD : (h + 1) * HD] = d_k
        dv_ref[:, h * HD : (h + 1) * HD] = d_v
    cosine = cos_ref[...]
    sine = sin_ref[...]
    d_q = rope(dq_ref[...], cosine, sine, -1)
    d_k = rope(dk_ref[...], cosine, sine, -1)
    d_v = dv_ref[...]
    d_normed = jnp.zeros(dmid.shape, F32)
    for c in range(count):
        rc = lax.rem(at - c + count, count)
        q_span = slice(c * qw, (c + 1) * qw)
        k_span = slice(c * kw, (c + 1) * kw)
        piece_ref[:, :qw] = d_q[:, q_span]
        piece_ref[:, qw : qw + kw] = d_k[:, k_span]
        piece_ref[:, qw + kw :] = d_v[:, k_span]
        piece = piece_ref[...].astype(BF16)
        d_normed = d_normed + dot_nt(piece, w_ref[rc, :, : qw + 2 * kw])

        @pl.when(at == c)
        def _():
            dqkv_ref[...] = piece

    u = u_ref[...].astype(F32)
    inv_a = lax.rsqrt(jnp.mean(u * u, axis=-1, keepdims=True) + epsilon)
    scaled = d_normed * gain_ref[0:1, :]
    d_in = dmid.astype(F32) + inv_a * scaled - u * (inv_a * inv_a * inv_a) * jnp.mean(
        scaled * u, axis=-1, keepdims=True
    )
    din_ref[...] = d_in.astype(BF16)
    gsum_ref[...] = jnp.sum((d_normed * u * inv_a)[:own], axis=0, keepdims=True)


def sds(shape, kind):
    return jax.ShapeDtypeStruct(shape, kind)


def specs(memory, operands):
    return [pl.BlockSpec(memory_space=memory)] + [pl.BlockSpec(memory_space=pltpu.VMEM)] * operands


LIMIT = pltpu.CompilerParams(vmem_limit_bytes=60 * 1024 * 1024)


def run_forward(at, u, weights, gate, up, down, gains, tables):
    t, width = u.shape
    ff = gate.shape[1]
    outs = (
        sds((t, width), BF16), sds((t, width), BF16), sds((t, HQ * HD), BF16), sds((t, KV * HD), BF16),
        sds((t, KV * HD), BF16), sds((HQ, t, t), BF16), sds((t, HQ * HD), BF16), sds((t, width), F32),
        sds((t, width), BF16), sds((t, ff), F32), sds((t, ff), F32), sds((t, ff), BF16),
    )
    return pl.pallas_call(
        forward_kernel,
        out_shape=outs,
        in_specs=specs(pltpu.SMEM, 12),
        scratch_shapes=[pltpu.VMEM((t, HQ * HD), F32), pltpu.VMEM((t, KV * HD), F32)],
        compiler_params=LIMIT,
        name="layer_forward",
    )(at, u, weights, gate, up, down, gains, *tables)


def run_ffn_back(upstream, gpre, upre, gate, up, down):
    t, width = upstream.shape
    ff = gate.shape[1]
    return pl.pallas_call(
        ffn_back_kernel,
        out_shape=(sds((t, 2 * ff), BF16), sds((t, width), BF16)),
        compiler_params=LIMIT,
        name="ffn_backward",
    )(upstream, gpre, upre, gate, up, down)


def run_attn_back(at, dmid, u, weights, gains, cosine, sine, q, k, v, prob, att, own):
    t, width = u.shape
    count = weights.shape[0]
    return pl.pallas_call(
        functools.partial(attn_back_kernel, own=own),
        out_shape=(
            sds((t, width), BF16), sds((t, (HQ + 2 * KV) * HD // count), BF16),
            sds((t, width // count), BF16), sds((1, width), F32),
        ),
        in_specs=specs(pltpu.SMEM, 11),
        scratch_shapes=[
            pltpu.VMEM((t, HQ * HD), BF16), pltpu.VMEM((t, HQ * HD), F32),
            pltpu.VMEM((t, KV * HD), F32), pltpu.VMEM((t, KV * HD), F32),
            pltpu.VMEM((t, (HQ + 2 * KV) * HD // count), F32),
        ],
        compiler_params=LIMIT,
        name="attention_backward",
    )(at, dmid, u, weights, gains, cosine, sine, q, k, v, prob, att)


def from_ahead(block, step, axis="shard"):
    n = lax.axis_size(axis)
    return lax.ppermute(block, axis, [(i, (i - step) % n) for i in range(n)])


def to_ahead(block, step, axis="shard"):
    n = lax.axis_size(axis)
    return lax.ppermute(block, axis, [(i, (i + step) % n) for i in range(n)])


def swap_section(block):
    return lax.ppermute(block, "section", [(0, 1), (1, 0)])


def gather_blocks(block):
    n = lax.axis_size("shard")
    return [block] + [from_ahead(block, i) for i in range(1, n)]


def gather_rows(block):
    return jnp.concatenate(gather_blocks(block), axis=0)


def scatter_rows(part):
    n = lax.axis_size("shard")
    size = part.shape[0] // n
    got = [to_ahead(part[i * size : (i + 1) * size], i) for i in range(1, n)]
    total = part[:size].astype(F32)
    for piece in got:
        total = total + piece.astype(F32)
    return total


def doubled_sum(block, axis):
    n = lax.axis_size(axis)
    step = 1
    while step < n:
        block = block + lax.ppermute(block, axis, [(i, i ^ step) for i in range(n)])
        step *= 2
    return block


def reduce_grad(partial, layer):
    n = lax.axis_size("replica")
    at = lax.axis_index("replica")
    other = lax.ppermute(partial, "section", [(1 - layer, layer)])
    total = partial.astype(F32) + other.astype(F32)
    rows = total.shape[0] // n
    if n > 4:
        return lax.psum_scatter(total.astype(BF16), "replica", scatter_dimension=0, tiled=True).astype(F32)
    sent = total.astype(BF16)
    result = lax.dynamic_slice_in_dim(sent, at * rows, rows, 0).astype(F32)
    for step in range(1, n):
        chunk = lax.dynamic_slice_in_dim(sent, lax.rem(at + step, n) * rows, rows, 0)
        route = [(layer * n + i, layer * n + (i + step) % n) for i in range(n)]
        result = result + lax.ppermute(chunk, ("section", "replica"), route).astype(F32)
    return result


def local(inputs, cotangent, segments, attn_q, attn_k, attn_v, attn_out, ffn_gate, ffn_up, ffn_down, norm_gains):
    section = lax.axis_index("section")
    shard = lax.axis_index("shard")
    n = lax.axis_size("shard")
    block = inputs.shape[1]
    width = inputs.shape[2]
    row_len = segments.shape[1]
    first = section == 0
    at = jnp.reshape(shard, (1,)).astype(jnp.int32)

    def by_layer(mine):
        other = swap_section(mine)
        return (jnp.where(first, mine, other), jnp.where(first, other, mine))

    x_own = lax.dynamic_index_in_dim(inputs, section, 0, keepdims=False)
    cot_own = lax.dynamic_index_in_dim(cotangent, section, 0, keepdims=False)
    seg = lax.dynamic_index_in_dim(segments, section, 0, keepdims=False)

    packed = by_layer(jnp.concatenate([attn_q[0], attn_k[0], attn_v[0], attn_out[0]], axis=1))
    half = width // 2

    def gather_weights(shard_l):
        mine = lax.dynamic_slice_in_dim(shard_l, section * half, half, 0)
        got = jnp.stack([to_ahead(mine, r) for r in range(1, n)])
        other = swap_section(got)
        low = jnp.where(first, got, other)
        high = jnp.where(first, other, got)
        return jnp.concatenate([shard_l[None], jnp.concatenate([low, high], axis=1)], axis=0)

    gains = by_layer(norm_gains[0])
    gates = by_layer(ffn_gate[0])
    ups = by_layer(ffn_up[0])
    downs = by_layer(ffn_down[0])
    u0 = gather_rows(x_own)
    weights = [gather_weights(packed[0]), gather_weights(packed[1])]
    cot = gather_rows(cot_own)

    index = jnp.arange(row_len, dtype=jnp.int32)
    pos = lax.rem(index + shard * block, row_len)
    seg_turned = lax.dynamic_slice_in_dim(jnp.concatenate([seg, seg]), shard * block, row_len, 0)
    start = jnp.sum((seg[None, :] < seg_turned[:, None]).astype(jnp.int32), axis=1)
    places = (pos - start).astype(F32)
    lane = jnp.arange(2 * HD, dtype=jnp.int32)
    frequency = rope_base ** ((lane % (HD // 2)).astype(F32) * (-2.0 / HD))
    angles = places[:, None] * frequency[None, :]
    cosine = jnp.cos(angles)
    sine = jnp.where((lane % HD < HD // 2)[None, :], -jnp.sin(angles), jnp.sin(angles))
    tables = (cosine, sine, seg_turned[:, None], pos[:, None], seg_turned[None, :], pos[None, :])

    us = [u0, None]
    saved = []
    acts = []
    for layer in range(2):
        kept = run_forward(at, us[layer], weights[layer], gates[layer], ups[layer], downs[layer], gains[layer], tables)
        saved.append(kept)
        own_out = (kept[7][:block] + scatter_rows(kept[0])).astype(BF16)
        acts.append(own_out)
        if layer == 0:
            us[1] = gather_rows(own_out)

    upstream = cot
    upstream_own = cot_own
    grads = [None, None]
    gain_parts = [None, None]
    d_inputs = [None, None]
    for layer in (1, 0):
        _, normed, q, k, v, prob, att, mid, nffn, gpre, upre, hid = saved[layer]
        dgu, part = run_ffn_back(upstream, gpre, upre, gates[layer], ups[layer], downs[layer])
        d_nffn = scatter_rows(part)
        mid_own = mid[:block]
        inv_f = lax.rsqrt(jnp.mean(mid_own * mid_own, axis=-1, keepdims=True) + epsilon)
        scaled = d_nffn * gains[layer][1]
        d_mid_own = (
            upstream_own.astype(F32)
            + inv_f * scaled
            - mid_own * (inv_f * inv_f * inv_f) * jnp.mean(scaled * mid_own, axis=-1, keepdims=True)
        ).astype(BF16)
        gain_ffn = jnp.sum(d_nffn * mid_own * inv_f, axis=0, keepdims=True)
        d_mid = gather_rows(d_mid_own)
        g_ffn = jnp.concatenate([dot_tn(nffn, dgu), dot_tn(upstream, hid)], axis=1).astype(BF16)
        red_ffn = reduce_grad(g_ffn, layer)
        d_in, dqkv, dmo, gain_attn = run_attn_back(
            at, d_mid, us[layer], weights[layer], gains[layer], cosine, sine, q, k, v, prob, att, block
        )
        g_attn = jnp.concatenate([dot_tn(normed, dqkv), dot_tn(att, dmo)], axis=1).astype(BF16)
        red_attn = reduce_grad(g_attn, layer)
        grads[layer] = (red_ffn, red_attn)
        gain_parts[layer] = jnp.concatenate([gain_attn, gain_ffn], axis=0)
        upstream = d_in
        upstream_own = d_in[:block]
        d_inputs[layer] = upstream_own

    gain_sum = jnp.concatenate(gain_parts, axis=0)
    for axis in ("section", "shard", "replica"):
        gain_sum = doubled_sum(gain_sum, axis)
    final_gains = jnp.where(first, gain_sum[:2], gain_sum[2:])
    red_ffn = jnp.where(first, grads[0][0], grads[1][0])
    red_attn = jnp.where(first, grads[0][1], grads[1][1])
    ff = ffn_gate.shape[2]
    qw = attn_q.shape[2]
    kw = attn_k.shape[2]

    def both_rows(pair):
        other = swap_section(jnp.where(first, pair[1], pair[0]))
        mine = jnp.where(first, pair[0], pair[1])
        return jnp.where(first, jnp.stack([mine, other]), jnp.stack([other, mine]))

    return (
        both_rows(acts)[None],
        both_rows(d_inputs)[None],
        red_attn[None, :, :qw],
        red_attn[None, :, qw : qw + kw],
        red_attn[None, :, qw + kw : qw + 2 * kw],
        red_attn[None, :, qw + 2 * kw :],
        red_ffn[None, :, :ff],
        red_ffn[None, :, ff : 2 * ff],
        red_ffn[:, 2 * ff :].T[None],
        final_gains[None],
    )


def solution(mesh):
    placed = (
        P("replica", "shard", None),
        P("replica", "shard", None),
        P("replica", None),
        P("section", None, "shard"),
        P("section", None, "shard"),
        P("section", None, "shard"),
        P("section", None, "shard"),
        P("section", None, "shard"),
        P("section", None, "shard"),
        P("section", "shard", None),
        P("section", None, None),
    )
    return jax.shard_map(
        local,
        mesh=mesh,
        in_specs=placed,
        out_specs=(
            P("section", "replica", "shard", None),
            P("section", "replica", "shard", None),
            P("section", "replica", "shard"),
            P("section", "replica", "shard"),
            P("section", "replica", "shard"),
            P("section", "replica", "shard"),
            P("section", "replica", "shard"),
            P("section", "replica", "shard"),
            P("section", "shard", "replica"),
            P("section", None, None),
        ),
        check_vma=False,
    )
```

time: 1160 us -> 415 us (0.36)
  waiting for transfers between devices: 626 us -> 110 us
  blocking collectives: 191 us -> 0 us
  matrix products: 113 us -> 8.88 us
  starting transfers between devices: 8.06 us -> 108 us
  local copies, waits for them, and re-layouts: 136 us -> 40 us
  Pallas kernels: 0 us -> 68.9 us
  other arithmetic: 53.3 us -> 72.7 us
  between operations: 16.7 us -> 2.1 us
    reduce_scatter x16 -> x0, waiting for transfers between devices: 441 us -> none  [the longest x3 84.2 us: local(): lax.psum_scatter(matmul(hidden, weight_down), 'shard', scatter_dimension=...]
    all_gather x14 -> x0, blocking collectives: 149 us -> none  [the longest x3 31 us: local(): grad_rows = lax.all_gather(upstream, 'shard', axis=0, tiled=True)]
    unnamed x32 -> x0, waiting for transfers between devices: 132 us -> none
    ppermute x4 -> x63, waiting for transfers between devices: 3.89 us -> 110 us  [the longest x12 52.7 us: reduce_grad(): lax.ppermute(chunk, ('section', 'replica'), route).astype(F32)]
    dot_general x70 -> x8, matrix products: 113 us -> 8.88 us  [dot_tn(): lax.dot_general(left, right, (((0,), (0,)), ((), ())), preferred_element_...]
    ppermute x4 -> x63, starting transfers between devices: 6.39 us -> 108 us  [the longest x12 43.1 us: reduce_grad(): lax.ppermute(chunk, ('section', 'replica'), route).astype(F32)]
    pallas_call x0 -> x6, Pallas kernels: none -> 68.9 us  [the longest x2 30.3 us: run_attn_back(): pl.pallas_call(functools.partial(attn_back_kernel, own=own), out_shape=(s...]
    all_gather x2 -> x0, waiting for transfers between devices: 48.6 us -> none  [the longest x1 46.4 us: local(): lax.all_gather(attn_out[0], 'shard', axis=1, tiled=True)]
  transfers between devices with their start and end apart: 29 -> 63, of which waited for: 24 -> 20; matrix products, arithmetic and copies ran while one was open for 14% -> 25% of each run, Pallas kernels for 0% -> 13%
where the time goes in v1:
time: 415 us; the launch traced here: 410 us
  waiting for transfers between devices  110 us (27%)
  starting transfers between devices  108 us (26%)
  other arithmetic  72.7 us (18%)
  Pallas kernels  68.9 us (17%)
  local copies, waits for them, and re-layouts  40 us (10%)
  matrix products  8.88 us (2%)
    ppermute x12, waiting for transfers between devices, reduce_grad(): lax.ppermute(chunk, ('section', 'replica'), route).astype(F32)  52.7 us
    ppermute x12, starting transfers between devices, reduce_grad(): lax.ppermute(chunk, ('section', 'replica'), route).astype(F32)  43.1 us
    ppermute x15, waiting for transfers between devices, from_ahead(): return lax.ppermute(block, axis, [(i, (i - step) % n) for i in range(n)])  34.4 us
    pallas_call x2, Pallas kernels, run_attn_back(): pl.pallas_call(functools.partial(attn_back_kernel, own=own), out_shape=(s...  30.3 us
    pallas_call x2, Pallas kernels, run_forward(): pl.pallas_call(forward_kernel, out_shape=outs, in_specs=specs(pltpu.SMEM,...  27.3 us
    ppermute x18, starting transfers between devices, to_ahead(): return lax.ppermute(block, axis, [(i, (i + step) % n) for i in range(n)])  22.9 us
    ppermute x15, starting transfers between devices, from_ahead(): return lax.ppermute(block, axis, [(i, (i - step) % n) for i in range(n)])  22.3 us
    ppermute x18, waiting for transfers between devices, to_ahead(): return lax.ppermute(block, axis, [(i, (i + step) % n) for i in range(n)])  19.4 us
  transfers between devices with their start and end apart: 63, of which 20 were waited for; matrix products, arithmetic and copies ran while one was open for 25% of the time, Pallas kernels for 13%

profile of v1, /device:TPU:0, one launch (start us, length us, event | category | flops | bytes accessed | tf_op | source)
XLA Modules:
  0.0 410.2 jit_solution(6374294069253402704)
XLA Ops:
  20.1 13.3 %collective-permute-done.28 = bf16[64,960]{1,0:T(8,128)(2,1)S(1)} collective-permute-done((bf16[64,960]{1,0:T(8,128)(2,1)S(1)}, bf16[64,960]{1,0:T(8,128)(2,1)S(1)}, u32[]{:S(2)}, u32[]{:S(2)}) %collective-permute-start.28) | collective-permute-done | bytes 122912 | tf_op jit(solution)/shard_map/ppermute | solution.py:249
  36.3 14.7 %collective-permute-done.27 = bf16[64,960]{1,0:T(8,128)(2,1)S(1)} collective-permute-done((bf16[64,960]{1,0:T(8,128)(2,1)S(1)}, bf16[64,960]{1,0:T(8,128)(2,1)S(1)}, u32[]{:S(2)}, u32[]{:S(2)}) %collective-permute-start.27) | collective-permute-done | bytes 122912 | tf_op jit(solution)/shard_map/ppermute | solution.py:249
  54.9 11.3 %collective-permute-done.20 = bf16[480,640]{1,0:T(8,128)(2,1)} collective-permute-done((bf16[480,640]{1,0:T(8,128)(2,1)}, bf16[480,640]{1,0:T(8,128)(2,1)}, u32[]{:S(2)}, u32[]{:S(2)}) %collective-permute-start.20) | collective-permute-done | bytes 614432 | tf_op jit(solution)/shard_map/ppermute | solution.py:254
  67.3 2.5 copy.55
  75.1 6.4 %collective-permute-done.18 = bf16[480,640]{1,0:T(8,128)(2,1)} collective-permute-done((bf16[480,640]{1,0:T(8,128)(2,1)}, bf16[480,640]{1,0:T(8,128)(2,1)}, u32[]{:S(2)}, u32[]{:S(2)}) %collective-permute-start.18) | collective-permute-done | bytes 614432 | tf_op jit(solution)/shard_map/ppermute | solution.py:254
  81.5 2.9 pad_maximum_fusion.3
  84.5 3.3 broadcast_select_fusion.5
  90.3 3.5 broadcast_select_fusion.4
  97.5 2.7 maximum_maximum_fusion.w_ref
  100.1 13.7 %layer_forward.2 = (bf16[256,960]{1,0:T(8,128)(2,1)}, bf16[256,960]{1,0:T(8,128)(2,1)}, bf16[256,960]{1,0:T(8,128)(2,1)}, bf16[256,320]{1,0:T(8,128)(2,1)}, bf16...) custom-call(s32[1]{0:T(128)} %bitcast.at_ref, ...), custom_call_target="tpu_custom_call" | custom-call | tf_op jit(solution)/shard_map/layer_forward/pallas_call | solution.py:206
  114.9 7.8 %collective-permute-start.14 = (bf16[64,960]{1,0:T(8,128)(2,1)S(1)}, bf16[64,960]{1,0:T(8,128)(2,1)S(1)}, u32[]{:S(2)}, u32[]{:S(2)}) collective-permute-start(bf16[64,960]{1,0:T(8,128)(2,1)S(1)} %get-tuple-element.173), channel_id=1, source_target_pairs={{0,12},{4,0},{8,4},{12,8},{1,13},{5,1},{9,5},{13,9},{2,14},{6,2},{... | collective-permute-start | bytes 368648 | tf_op jit(solution)/shard_map/ppermute | solution.py:254
  126.2 2.7 maximum_maximum_fusion.1.w_ref
  136.0 2.6 collective-permute-done.17
  140.1 13.6 %layer_forward.3 = (bf16[256,960]{1,0:T(8,128)(2,1)}, bf16[256,960]{1,0:T(8,128)(2,1)}, bf16[256,960]{1,0:T(8,128)(2,1)}, bf16[256,320]{1,0:T(8,128)(2,1)}, bf16...) custom-call(s32[1]{0:T(128)} %bitcast.at_ref, ...), custom_call_target="tpu_custom_call" | custom-call | tf_op jit(solution)/shard_map/layer_forward/pallas_call | solution.py:206
  160.0 5.7 %ffn_backward.2 = (bf16[256,1280]{1,0:T(8,128)(2,1)}, bf16[256,960]{1,0:T(8,128)(2,1)}) custom-call(bf16[256,960]{1,0:T(8,128)(2,1)} %pad_maximum_fusion.9.g_ref, f32[256,640]{1,0:T(8,128)} %get-tuple-element.50.gpre_ref, f32[256,640]{1,0:T(8,128)} %get-tuple-element.51.upre_ref, bf16[960,640]{1,0:T(8,128)(2,1)} %get-tuple-element.142.gate_ref, ...), custom_call_target="tpu_custom_call" | custom-call | tf_op jit(solution)/shard_map/ffn_backward/pallas_call | solution.py:219
  175.5 3.2 collective-permute-start.54
  188.0 15.1 %attention_backward.2 = (bf16[256,960]{1,0:T(8,128)(2,1)}, bf16[256,400]{1,0:T(8,128)(2,1)}, bf16[256,240]{1,0:T(8,128)(2,1)}, f32[1,960]{1,0:T(1,128)}) custom-call(s32[1]{0:T(128)} %bitcast.at_ref, bf16[256,960]{1,0:T(8,128)(2,1)} %pad_maximum_fusion.10.dmid_ref, bf16[256,960]{1,0:T(8,128)(2,1)} %pad_maximum_fusion.8.u_ref, ...), custom_call_target="tpu_custom_call" | custom-call | tf_op jit(solution)/shard_map/attention_backward/pallas_call | solution.py:230
  203.1 5.7 %ffn_backward.3 = (bf16[256,1280]{1,0:T(8,128)(2,1)}, bf16[256,960]{1,0:T(8,128)(2,1)}) custom-call(bf16[256,960]{1,0:T(8,128)(2,1)} %get-tuple-element.58.g_ref, f32[256,640]{1,0:T(8,128)} %get-tuple-element.59.gpre_ref, f32[256,640]{1,0:T(8,128)} %get-tuple-element.60.upre_ref, bf16[960,640]{1,0:T(8,128)(2,1)} %get-tuple-element.143.gate_ref, ...), custom_call_target="tpu_custom_call" | custom-call | tf_op jit(solution)/shard_map/ffn_backward/pallas_call | solution.py:219
  228.0 2.6 collective-permute-start.40
  237.1 15.2 %attention_backward.3 = (bf16[256,960]{1,0:T(8,128)(2,1)}, bf16[256,400]{1,0:T(8,128)(2,1)}, bf16[256,240]{1,0:T(8,128)(2,1)}, f32[1,960]{1,0:T(1,128)}) custom-call(s32[1]{0:T(128)} %bitcast.at_ref, bf16[256,960]{1,0:T(8,128)(2,1)} %pad_maximum_fusion.11.dmid_ref, bf16[256,960]{1,0:T(8,128)(2,1)} %pad_maximum_fusion.7.u_ref, ...), custom_call_target="tpu_custom_call" | custom-call | tf_op jit(solution)/shard_map/attention_backward/pallas_call | solution.py:230
  276.4 2.6 collective-permute-start.62
  281.1 2.5 copy.66
  297.2 2.5 add_convert_fusion
  301.6 5.7 %collective-permute-start.45 = (bf16[240,640]{0,1:T(8,128)(2,1)S(1)}, bf16[240,640]{0,1:T(8,128)(2,1)S(1)}, u32[]{:S(2)}, u32[]{:S(2)}) collective-permute-start(bf16[240,640]{0,1:T(8,128)(2,1)S(1)} %get-tuple-element.150), channel_id=1, source_target_pairs={{0,3},{1,0},{2,1},{3,2},{4,7},{5,4},{6,5},{7,6},{8,11},{9,8},{10,9... | collective-permute-start | bytes 921608 | tf_op jit(solution)/shard_map/ppermute | solution.py:302
  309.2 2.8 collective-permute-start.43
  312.9 2.5 add_convert_fusion.1
  321.2 7.3 %collective-permute-done.44 = bf16[240,640]{0,1:T(8,128)(2,1)S(1)} collective-permute-done((bf16[240,640]{0,1:T(8,128)(2,1)S(1)}, bf16[240,640]{0,1:T(8,128)(2,1)S(1)}, u32[]{:S(2)}, u32[]{:S(2)}) %collective-permute-start.44) | collective-permute-done | bytes 307232 | tf_op jit(solution)/shard_map/ppermute | solution.py:302
  328.6 17.1 %collective-permute-start.53 = (bf16[240,1920]{1,0:T(8,128)(2,1)}, bf16[240,1920]{1,0:T(8,128)(2,1)}, u32[]{:S(2)}, u32[]{:S(2)}) collective-permute-start(bf16[240,1920]{1,0:T(8,128)(2,1)} %get-tuple-element.129), channel_id=1, source_target_pairs={{0,3},{1,0},{2,1},{3,2},{4,7},{5,4},{6,5},{7,6},{8,11},{9,8},{10,9... | collective-permute-start | bytes 2764808 | tf_op jit(solution)/shard_map/ppermute | solution.py:302
  345.7 6.0 %collective-permute-start.52 = (bf16[240,1920]{1,0:T(8,128)(2,1)}, bf16[240,1920]{1,0:T(8,128)(2,1)}, u32[]{:S(2)}, u32[]{:S(2)}) collective-permute-start(bf16[240,1920]{1,0:T(8,128)(2,1)} %get-tuple-element.130), channel_id=1, source_target_pairs={{0,2},{1,3},{2,0},{3,1},{4,6},{5,7},{6,4},{7,5},{8,10},{9,11},{10,... | collective-permute-start | bytes 2764808 | tf_op jit(solution)/shard_map/ppermute | solution.py:302
  359.0 4.0 collective-permute-done.53
  363.1 41.3 %collective-permute-done.52 = bf16[240,1920]{1,0:T(8,128)(2,1)} collective-permute-done((bf16[240,1920]{1,0:T(8,128)(2,1)}, bf16[240,1920]{1,0:T(8,128)(2,1)}, u32[]{:S(2)}, u32[]{:S(2)}) %collective-permute-start.52) | collective-permute-done | bytes 921632 | tf_op jit(solution)/shard_map/ppermute | solution.py:302
  404.4 4.0 add_select_fusion
  (305 shorter events, 161.1 us)
Async XLA Ops:
  14.3 37.1 %collective-permute-start.6 = (bf16[480,640]{1,0:T(8,128)(2,1)S(1)}, bf16[480,640]{1,0:T(8,128)(2,1)S(1)}, u32[]{:S(2)}, u32[]{:S(2)}) collective-permute-start(bf16[480,640]{1,0:T(8,128)(2,1)S(1)} %constant_dynamic-slice_fusion.14), channel_id=1, source_target_pairs={{0,12},{4,0},{8,4},{12,8},{1,13},{5,1},{9,5},{13,9},{2,14},{6,2},{... | collective-permute-start | bytes 1843208 | tf_op jit(solution)/shard_map/ppermute | solution.py:254
  14.9 18.5 %collective-permute-start.28 = (bf16[64,960]{1,0:T(8,128)(2,1)S(1)}, bf16[64,960]{1,0:T(8,128)(2,1)S(1)}, u32[]{:S(2)}, u32[]{:S(2)}) collective-permute-start(bf16[64,960]{1,0:T(8,128)(2,1)S(1)} %dynamic-slice_bitcast_fusion), channel_id=1, source_target_pairs={{0,4},{4,8},{8,12},{12,0},{1,5},{5,9},{9,13},{13,1},{2,6},{6,10},{... | collective-permute-start | bytes 368648 | tf_op jit(solution)/shard_map/ppermute | solution.py:249
  16.5 36.3 %collective-permute-start.5 = (bf16[480,640]{1,0:T(8,128)(2,1)S(1)}, bf16[480,640]{1,0:T(8,128)(2,1)S(1)}, u32[]{:S(2)}, u32[]{:S(2)}) collective-permute-start(bf16[480,640]{1,0:T(8,128)(2,1)S(1)} %constant_dynamic-slice_fusion.14), channel_id=1, source_target_pairs={{0,8},{4,12},{8,0},{12,4},{1,9},{5,13},{9,1},{13,5},{2,10},{6,14},... | collective-permute-start | bytes 1843208 | tf_op jit(solution)/shard_map/ppermute | solution.py:254
  16.7 36.6 %collective-permute-start.4 = (bf16[480,640]{1,0:T(8,128)(2,1)S(1)}, bf16[480,640]{1,0:T(8,128)(2,1)S(1)}, u32[]{:S(2)}, u32[]{:S(2)}) collective-permute-start(bf16[480,640]{1,0:T(8,128)(2,1)S(1)} %constant_dynamic-slice_fusion.14), channel_id=1, source_target_pairs={{0,4},{4,8},{8,12},{12,0},{1,5},{5,9},{9,13},{13,1},{2,6},{6,10},{... | collective-permute-start | bytes 1843208 | tf_op jit(solution)/shard_map/ppermute | solution.py:254
  18.7 32.3 %collective-permute-start.27 = (bf16[64,960]{1,0:T(8,128)(2,1)S(1)}, bf16[64,960]{1,0:T(8,128)(2,1)S(1)}, u32[]{:S(2)}, u32[]{:S(2)}) collective-permute-start(bf16[64,960]{1,0:T(8,128)(2,1)S(1)} %dynamic-slice_bitcast_fusion), channel_id=1, source_target_pairs={{0,8},{4,12},{8,0},{12,4},{1,9},{5,13},{9,1},{13,5},{2,10},{6,14},... | collective-permute-start | bytes 368648 | tf_op jit(solution)/shard_map/ppermute | solution.py:249
  33.5 17.6 %collective-permute-start.26 = (bf16[64,960]{1,0:T(8,128)(2,1)S(1)}, bf16[64,960]{1,0:T(8,128)(2,1)S(1)}, u32[]{:S(2)}, u32[]{:S(2)}) collective-permute-start(bf16[64,960]{1,0:T(8,128)(2,1)S(1)} %dynamic-slice_bitcast_fusion), channel_id=1, source_target_pairs={{0,12},{4,0},{8,4},{12,8},{1,13},{5,1},{9,5},{13,9},{2,14},{6,2},{... | collective-permute-start | bytes 368648 | tf_op jit(solution)/shard_map/ppermute | solution.py:249
  51.0 15.8 %collective-permute-start.19 = (bf16[480,640]{1,0:T(8,128)(2,1)}, bf16[480,640]{1,0:T(8,128)(2,1)}, u32[]{:S(2)}, u32[]{:S(2)}) collective-permute-start(bf16[480,640]{1,0:T(8,128)(2,1)} %constant_dynamic-slice_fusion.12), channel_id=1, source_target_pairs={{0,8},{4,12},{8,0},{12,4},{1,9},{5,13},{9,1},{13,5},{2,10},{6,14},... | collective-permute-start | bytes 1843208 | tf_op jit(solution)/shard_map/ppermute | solution.py:254
  51.4 33.0 %collective-permute-start.8 = (bf16[960,640]{1,0:T(8,128)(2,1)}, bf16[960,640]{1,0:T(8,128)(2,1)}, u32[]{:S(2)}, u32[]{:S(2)}) collective-permute-start(bf16[960,640]{1,0:T(8,128)(2,1)} %bitcast.10), channel_id=1, source_target_pairs={{0,16},{16,0},{1,17},{17,1},{2,18},{18,2},{3,19},{19,3},{4,20},{20... | collective-permute-start | bytes 3686408 | tf_op jit(solution)/shard_map/ppermute | solution.py:258
  52.8 37.5 %collective-permute-start.9 = (bf16[960,640]{1,0:T(8,128)(2,1)}, bf16[960,640]{1,0:T(8,128)(2,1)}, u32[]{:S(2)}, u32[]{:S(2)}) collective-permute-start(bf16[960,640]{1,0:T(8,128)(2,1)} %bitcast.11), channel_id=1, source_target_pairs={{0,16},{16,0},{1,17},{17,1},{2,18},{18,2},{3,19},{19,3},{4,20},{20... | collective-permute-start | bytes 3686408 | tf_op jit(solution)/shard_map/ppermute | solution.py:258
  53.3 34.5 %collective-permute-start.10 = (bf16[640,960]{0,1:T(8,128)(2,1)}, bf16[640,960]{0,1:T(8,128)(2,1)}, u32[]{:S(2)}, u32[]{:S(2)}) collective-permute-start(bf16[640,960]{0,1:T(8,128)(2,1)} %bitcast.13), channel_id=1, source_target_pairs={{0,16},{16,0},{1,17},{17,1},{2,18},{18,2},{3,19},{19,3},{4,20},{20... | collective-permute-start | bytes 3686408 | tf_op jit(solution)/shard_map/ppermute | solution.py:258
  66.2 15.4 %collective-permute-start.18 = (bf16[480,640]{1,0:T(8,128)(2,1)}, bf16[480,640]{1,0:T(8,128)(2,1)}, u32[]{:S(2)}, u32[]{:S(2)}) collective-permute-start(bf16[480,640]{1,0:T(8,128)(2,1)} %constant_dynamic-slice_fusion.12), channel_id=1, source_target_pairs={{0,4},{4,8},{8,12},{12,0},{1,5},{5,9},{9,13},{13,1},{2,6},{6,10},{... | collective-permute-start | bytes 1843208 | tf_op jit(solution)/shard_map/ppermute | solution.py:254
  66.8 28.7 %collective-permute-start.7 = (bf16[3,480,640]{2,1,0:T(8,128)(2,1)}, bf16[3,480,640]{2,1,0:T(8,128)(2,1)}, u32[]{:S(2)}, u32[]{:S(2)}) collective-permute-start(bf16[3,480,640]{2,1,0:T(8,128)(2,1)} %pad_maximum_fusion.2), channel_id=1, source_target_pairs={{0,16},{16,0},{1,17},{17,1},{2,18},{18,2},{3,19},{19,3},{4,20},{20... | collective-permute-start | bytes 5529608 | tf_op jit(solution)/shard_map/ppermute | solution.py:258
  84.5 39.2 %collective-permute-start.21 = (bf16[3,480,640]{2,1,0:T(8,128)(2,1)}, bf16[3,480,640]{2,1,0:T(8,128)(2,1)}, u32[]{:S(2)}, u32[]{:S(2)}) collective-permute-start(bf16[3,480,640]{2,1,0:T(8,128)(2,1)} %pad_maximum_fusion.3), channel_id=1, source_target_pairs={{0,16},{16,0},{1,17},{17,1},{2,18},{18,2},{3,19},{19,3},{4,20},{20... | collective-permute-start | bytes 5529608 | tf_op jit(solution)/shard_map/ppermute | solution.py:258
  155.5 25.6 %collective-permute-start.24 = (bf16[64,960]{1,0:T(8,128)(2,1)}, bf16[64,960]{1,0:T(8,128)(2,1)S(1)}, u32[]{:S(2)}, u32[]{:S(2)}) collective-permute-start(bf16[64,960]{1,0:T(8,128)(2,1)} %get-tuple-element.170), channel_id=1, source_target_pairs={{0,12},{4,0},{8,4},{12,8},{1,13},{5,1},{9,5},{13,9},{2,14},{6,2},{... | collective-permute-start | bytes 368648 | tf_op jit(solution)/shard_map/ppermute | solution.py:254
  158.0 24.2 %collective-permute-start.23 = (bf16[64,960]{1,0:T(8,128)(2,1)S(1)}, bf16[64,960]{1,0:T(8,128)(2,1)S(1)}, u32[]{:S(2)}, u32[]{:S(2)}) collective-permute-start(bf16[64,960]{1,0:T(8,128)(2,1)S(1)} %get-tuple-element.171), channel_id=1, source_target_pairs={{0,8},{4,12},{8,0},{12,4},{1,9},{5,13},{9,1},{13,5},{2,10},{6,14},... | collective-permute-start | bytes 368648 | tf_op jit(solution)/shard_map/ppermute | solution.py:254
  175.5 120.4 %collective-permute-start.54 = (bf16[960,1920]{1,0:T(8,128)(2,1)}, bf16[960,1920]{1,0:T(8,128)(2,1)}, u32[]{:S(2)}, u32[]{:S(2)}) collective-permute-start(bf16[960,1920]{1,0:T(8,128)(2,1)} %pad_maximum_fusion.1), channel_id=1, source_target_pairs={{0,16},{1,17},{2,18},{3,19},{4,20},{5,21},{6,22},{7,23},{8,24},{9,... | collective-permute-start | bytes 11059208 | tf_op jit(solution)/shard_map/ppermute | solution.py:292
  218.5 62.6 %collective-permute-start.46 = (bf16[960,640]{1,0:T(8,128)(2,1)}, bf16[960,640]{1,0:T(8,128)(2,1)}, u32[]{:S(2)}, u32[]{:S(2)}) collective-permute-start(bf16[960,640]{1,0:T(8,128)(2,1)} %copy.65), channel_id=1, source_target_pairs={{0,16},{1,17},{2,18},{3,19},{4,20},{5,21},{6,22},{7,23},{8,24},{9,... | collective-permute-start | bytes 3686408 | tf_op jit(solution)/shard_map/ppermute | solution.py:292
  234.2 77.9 %collective-permute-start.50 = (bf16[960,1920]{1,0:T(8,128)(2,1)}, bf16[960,1920]{1,0:T(8,128)(2,1)}, u32[]{:S(2)}, u32[]{:S(2)}) collective-permute-start(bf16[960,1920]{1,0:T(8,128)(2,1)} %pad_maximum_fusion), channel_id=1, source_target_pairs={{16,0},{17,1},{18,2},{19,3},{20,4},{21,5},{22,6},{23,7},{24,8},{25... | collective-permute-start | bytes 11059208 | tf_op jit(solution)/shard_map/ppermute | solution.py:292
  264.6 24.8 %collective-permute-start.42 = (bf16[960,640]{1,0:T(8,128)(2,1)}, bf16[960,640]{1,0:T(8,128)(2,1)}, u32[]{:S(2)}, u32[]{:S(2)}) collective-permute-start(bf16[960,640]{1,0:T(8,128)(2,1)} %copy.62), channel_id=1, source_target_pairs={{16,0},{17,1},{18,2},{19,3},{20,4},{21,5},{22,6},{23,7},{24,8},{25... | collective-permute-start | bytes 3686408 | tf_op jit(solution)/shard_map/ppermute | solution.py:292
  281.0 20.6 %collective-permute-start.41 = (bf16[64,960]{1,0:T(8,128)(2,1)}, bf16[64,960]{1,0:T(8,128)(2,1)S(1)}, u32[]{:S(2)}, u32[]{:S(2)}) collective-permute-start(bf16[64,960]{1,0:T(8,128)(2,1)} %get-tuple-element.156), channel_id=1, source_target_pairs={{0,16},{16,0},{1,17},{17,1},{2,18},{18,2},{3,19},{19,3},{4,20},{20... | collective-permute-start | bytes 368648 | tf_op jit(solution)/shard_map/ppermute | solution.py:258
  288.0 19.3 %collective-permute-start.49 = (bf16[240,640]{0,1:T(8,128)(2,1)}, bf16[240,640]{0,1:T(8,128)(2,1)}, u32[]{:S(2)}, u32[]{:S(2)}) collective-permute-start(bf16[240,640]{0,1:T(8,128)(2,1)} %get-tuple-element.153), channel_id=1, source_target_pairs={{16,19},{17,16},{18,17},{19,18},{20,23},{21,20},{22,21},{23,22},{2... | collective-permute-start | bytes 921608 | tf_op jit(solution)/shard_map/ppermute | solution.py:302
  289.4 19.8 %collective-permute-start.48 = (bf16[240,640]{0,1:T(8,128)(2,1)}, bf16[240,640]{0,1:T(8,128)(2,1)}, u32[]{:S(2)}, u32[]{:S(2)}) collective-permute-start(bf16[240,640]{0,1:T(8,128)(2,1)} %get-tuple-element.154), channel_id=1, source_target_pairs={{16,18},{17,19},{18,16},{19,17},{20,22},{21,23},{22,20},{23,21},{2... | collective-permute-start | bytes 921608 | tf_op jit(solution)/shard_map/ppermute | solution.py:302
  296.5 21.6 %collective-permute-start.47 = (bf16[240,640]{0,1:T(8,128)(2,1)S(1)}, bf16[240,640]{0,1:T(8,128)(2,1)S(1)}, u32[]{:S(2)}, u32[]{:S(2)}) collective-permute-start(bf16[240,640]{0,1:T(8,128)(2,1)S(1)} %copy-done.33), channel_id=1, source_target_pairs={{16,17},{17,18},{18,19},{19,16},{20,21},{21,22},{22,23},{23,20},{2... | collective-permute-start | bytes 921608 | tf_op jit(solution)/shard_map/ppermute | solution.py:302
  301.6 18.1 %collective-permute-start.45 = (bf16[240,640]{0,1:T(8,128)(2,1)S(1)}, bf16[240,640]{0,1:T(8,128)(2,1)S(1)}, u32[]{:S(2)}, u32[]{:S(2)}) collective-permute-start(bf16[240,640]{0,1:T(8,128)(2,1)S(1)} %get-tuple-element.150), channel_id=1, source_target_pairs={{0,3},{1,0},{2,1},{3,2},{4,7},{5,4},{6,5},{7,6},{8,11},{9,8},{10,9... | collective-permute-start | bytes 921608 | tf_op jit(solution)/shard_map/ppermute | solution.py:302
  307.3 21.3 %collective-permute-start.44 = (bf16[240,640]{0,1:T(8,128)(2,1)S(1)}, bf16[240,640]{0,1:T(8,128)(2,1)S(1)}, u32[]{:S(2)}, u32[]{:S(2)}) collective-permute-start(bf16[240,640]{0,1:T(8,128)(2,1)S(1)} %get-tuple-element.151), channel_id=1, source_target_pairs={{0,2},{1,3},{2,0},{3,1},{4,6},{5,7},{6,4},{7,5},{8,10},{9,11},{10,... | collective-permute-start | bytes 921608 | tf_op jit(solution)/shard_map/ppermute | solution.py:302
  309.2 36.4 %collective-permute-start.43 = (bf16[240,640]{0,1:T(8,128)(2,1)S(1)}, bf16[240,640]{0,1:T(8,128)(2,1)S(1)}, u32[]{:S(2)}, u32[]{:S(2)}) collective-permute-start(bf16[240,640]{0,1:T(8,128)(2,1)S(1)} %get-tuple-element.149), channel_id=1, source_target_pairs={{0,1},{1,2},{2,3},{3,0},{4,5},{5,6},{6,7},{7,4},{8,9},{9,10},{10,1... | collective-permute-start | bytes 921608 | tf_op jit(solution)/shard_map/ppermute | solution.py:302
  312.1 39.6 %collective-permute-start.57 = (bf16[240,1920]{1,0:T(8,128)(2,1)S(1)}, bf16[240,1920]{1,0:T(8,128)(2,1)S(1)}, u32[]{:S(2)}, u32[]{:S(2)}) collective-permute-start(bf16[240,1920]{1,0:T(8,128)(2,1)S(1)} %get-tuple-element.132), channel_id=1, source_target_pairs={{16,19},{17,16},{18,17},{19,18},{20,23},{21,20},{22,21},{23,22},{2... | collective-permute-start | bytes 2764808 | tf_op jit(solution)/shard_map/ppermute | solution.py:302
  318.0 41.0 %collective-permute-start.56 = (bf16[240,1920]{1,0:T(8,128)(2,1)S(1)}, bf16[240,1920]{1,0:T(8,128)(2,1)}, u32[]{:S(2)}, u32[]{:S(2)}) collective-permute-start(bf16[240,1920]{1,0:T(8,128)(2,1)S(1)} %get-tuple-element.133), channel_id=1, source_target_pairs={{16,18},{17,19},{18,16},{19,17},{20,22},{21,23},{22,20},{23,21},{2... | collective-permute-start | bytes 2764808 | tf_op jit(solution)/shard_map/ppermute | solution.py:302
  319.6 39.4 %collective-permute-start.55 = (bf16[240,1920]{1,0:T(8,128)(2,1)S(1)}, bf16[240,1920]{1,0:T(8,128)(2,1)}, u32[]{:S(2)}, u32[]{:S(2)}) collective-permute-start(bf16[240,1920]{1,0:T(8,128)(2,1)S(1)} %get-tuple-element.131), channel_id=1, source_target_pairs={{16,17},{17,18},{18,19},{19,16},{20,21},{21,22},{22,23},{23,20},{2... | collective-permute-start | bytes 2764808 | tf_op jit(solution)/shard_map/ppermute | solution.py:302
  328.6 34.5 %collective-permute-start.53 = (bf16[240,1920]{1,0:T(8,128)(2,1)}, bf16[240,1920]{1,0:T(8,128)(2,1)}, u32[]{:S(2)}, u32[]{:S(2)}) collective-permute-start(bf16[240,1920]{1,0:T(8,128)(2,1)} %get-tuple-element.129), channel_id=1, source_target_pairs={{0,3},{1,0},{2,1},{3,2},{4,7},{5,4},{6,5},{7,6},{8,11},{9,8},{10,9... | collective-permute-start | bytes 2764808 | tf_op jit(solution)/shard_map/ppermute | solution.py:302
  345.7 58.7 %collective-permute-start.52 = (bf16[240,1920]{1,0:T(8,128)(2,1)}, bf16[240,1920]{1,0:T(8,128)(2,1)}, u32[]{:S(2)}, u32[]{:S(2)}) collective-permute-start(bf16[240,1920]{1,0:T(8,128)(2,1)} %get-tuple-element.130), channel_id=1, source_target_pairs={{0,2},{1,3},{2,0},{3,1},{4,6},{5,7},{6,4},{7,5},{8,10},{9,11},{10,... | collective-permute-start | bytes 2764808 | tf_op jit(solution)/shard_map/ppermute | solution.py:302
  351.7 52.7 %collective-permute-start.51 = (bf16[240,1920]{1,0:T(8,128)(2,1)}, bf16[240,1920]{1,0:T(8,128)(2,1)}, u32[]{:S(2)}, u32[]{:S(2)}) collective-permute-start(bf16[240,1920]{1,0:T(8,128)(2,1)} %get-tuple-element.128), channel_id=1, source_target_pairs={{0,1},{1,2},{2,3},{3,0},{4,5},{5,6},{6,7},{7,4},{8,9},{9,10},{10,1... | collective-permute-start | bytes 2764808 | tf_op jit(solution)/shard_map/ppermute | solution.py:302
  (86 other events, 631.7 us)
